TPU v7x, 512 devices: a whole 4x4x16 slice. The times are simulated.
512 devices in a mesh: section: 2 (over x_hi), lat: 64 (over z, x_lo, core), tp: 4 (over y).
Axes of the slice: x: 4 (x_hi: 2, x_lo: 2; x = x_hi * 2 + x_lo), y: 4, z: 16, core: 2. Of those that a mesh axis runs over, the one named last changes fastest.
Arguments:
- initial_field: bfloat16 [2, 8, 192, 48, 192], P(None, 'tp', 'lat'), may hold values from -6 to 6
- first_gain: bfloat16 [2, 192], P('section'), may hold values from 0.25 to 1.75
- first_shift: bfloat16 [2, 192], P('section'), may hold values from -1.75 to 1.75
- qkv_weight: bfloat16 [2, 192, 576], P('section', None, 'tp'), may hold values from -0.4375 to 0.4375
- qkv_bias: bfloat16 [2, 576], P('section', 'tp'), may hold values from -1.75 to 1.75
- proj_weight: bfloat16 [2, 192, 192], P('section', None, 'tp'), may hold values from -0.4375 to 0.4375
- proj_bias: bfloat16 [2, 192], P('section', 'tp'), may hold values from -1.75 to 1.75
- second_gain: bfloat16 [2, 192], P('section'), may hold values from 0.25 to 1.75
- second_shift: bfloat16 [2, 192], P('section'), may hold values from -1.75 to 1.75
- expand_weight: bfloat16 [2, 192, 768], P('section', None, 'tp'), may hold values from -0.4375 to 0.4375
- expand_bias: bfloat16 [2, 768], P('section', 'tp'), may hold values from -1.75 to 1.75
- reduce_weight: bfloat16 [2, 768, 192], P('section', 'tp'), may hold values from -0.21875 to 0.21875
- reduce_bias: bfloat16 [2, 192], P('section', 'tp'), may hold values from -1.75 to 1.75
- earth_bias: float32 [2, 4, 64, 6, 1656], P('section', 'tp', 'lat'), may hold values from -4 to 340
Outputs:
- predicted_states: bfloat16 [2, 2, 8, 192, 48, 192], P('section', None, 'tp', 'lat')
All inputs are finite; a program needn't handle non-finite values.
Results may differ from a plain program's by a relative error of at most 0.018.
Values may be sent and summed in bfloat16 or wider, within the bound.
No kernel may reach another device: no remote copies, remote signals or barrier semaphores. Data moves between devices by JAX's collectives and lax.ppermute only.
A program may use at most 64 MiB of HBM per device.

v0:
```python
import jax
import jax.numpy as jnp
import numpy as np
from jax import lax
from jax.sharding import PartitionSpec as P

WZ = 2
WH = 6
WW = 12
epsilon = 1e-05


def swapped(block, axis, apart):
    count = lax.axis_size(axis)
    route = []
    for low in range(count):
        high = low | 1 << apart
        if high != low and high < count:
            route += [(low, high), (high, low)]
    return lax.ppermute(block, axis, route)


def passed_along(value, axis, steps):
    count = lax.axis_size(axis)
    first, last = (max(0, -steps), min(count, count - steps))
    return lax.ppermute(value, axis, [(source, source + steps) for source in range(first, last)])


def bias_entries():
    half_rows = WH // 2
    query_pos = np.arange(WZ * half_rows * WW)
    attended_location = np.arange(WZ * WH * WW)
    query_level = query_pos // (half_rows * WW)
    query_row = query_pos // WW % half_rows
    query_col = query_pos % WW
    key_level = attended_location // (WH * WW)
    key_row = attended_location // WW % WH
    key_column_index = attended_location % WW
    table_items = (
        ((query_level[:, None] * WZ + key_level[None, :]) * half_rows + query_row[:, None]) * WH
        + key_row[None, :]
    ) * (2 * WW - 1) + (query_col[:, None] - key_column_index[None, :] + WW - 1)
    return table_items.astype(np.int32)


def layer_norm(values, gain, offset):
    floats = values.astype(jnp.float32)
    middle_point = jnp.mean(floats, axis=-1, keepdims=True)
    spread = jnp.mean((floats - middle_point) ** 2, axis=-1, keepdims=True)
    return (floats - middle_point) * lax.rsqrt(spread + epsilon) * gain.astype(
        jnp.float32
    ) + offset.astype(jnp.float32)


def earth_block(grid, norms, weights, bias_block, band_half):
    first_gain, first_shift, second_gain, second_shift = norms
    (
        qkv_matrix,
        qkv_offset,
        proj_matrix,
        proj_offset,
        expand_matrix,
        expand_offset,
        reduce_matrix,
        shrink_translation,
    ) = weights
    levels, lat_rows, lon_cols, width = grid.shape
    heads = bias_block.shape[0]
    head_size = width // heads
    scale = 1.0 / float(np.sqrt(head_size))
    meridian_slabs = lon_cols // WW
    normed = layer_norm(grid, first_gain, first_shift).astype(jnp.bfloat16)
    flat = normed.reshape(-1, width)
    own_mixed = (
        jnp.dot(flat, qkv_matrix, preferred_element_type=jnp.float32)
        + qkv_offset.astype(jnp.float32)
    ).astype(jnp.bfloat16)
    neighbour_keyvalue = swapped(own_mixed[:, width:], "lat", 0)
    own_kv = own_mixed[:, width:].reshape(levels, lat_rows, lon_cols, 2 * width)
    neighbour_keyvalue = neighbour_keyvalue.reshape(levels, lat_rows, lon_cols, 2 * width)
    lower_first = jnp.concatenate([own_kv, neighbour_keyvalue], axis=1)
    upper_first = jnp.concatenate([neighbour_keyvalue, own_kv], axis=1)
    window_kv = jnp.where(band_half == 0, lower_first, upper_first)
    keyvals = window_kv.reshape(levels, 2 * lat_rows, meridian_slabs, WW, 2 * width).transpose(
        2, 0, 1, 3, 4
    )
    keyvals = keyvals.reshape(meridian_slabs, levels * 2 * lat_rows * WW, 2 * width)
    query_rows = (
        own_mixed[:, :width]
        .reshape(levels, lat_rows, meridian_slabs, WW, width)
        .transpose(2, 0, 1, 3, 4)
    )
    query_rows = query_rows.reshape(meridian_slabs, levels * lat_rows * WW, width)
    query_count = query_rows.shape[1]
    key_count = keyvals.shape[1]
    query_heads = query_rows.reshape(meridian_slabs, query_count, heads, head_size)
    key_heads = keyvals[..., :width].reshape(meridian_slabs, key_count, heads, head_size)
    value_heads = keyvals[..., width:].reshape(meridian_slabs, key_count, heads, head_size)
    scores = (
        jnp.einsum("wqhd,wkhd->whqk", query_heads, key_heads, preferred_element_type=jnp.float32)
        * scale
        + bias_block[None]
    )
    probs = jax.nn.softmax(scores, axis=-1).astype(jnp.bfloat16)
    attended = jnp.einsum(
        "whqk,wkhd->wqhd", probs, value_heads, preferred_element_type=jnp.float32
    ).astype(jnp.bfloat16)
    merged = (
        attended.reshape(meridian_slabs, levels, lat_rows, WW, width)
        .transpose(1, 2, 0, 3, 4)
        .reshape(-1, width)
    )
    branch = jnp.dot(merged, proj_matrix, preferred_element_type=jnp.float32) + proj_offset.astype(
        jnp.float32
    )
    middle = (grid.reshape(-1, width).astype(jnp.float32) + branch).astype(jnp.bfloat16)
    normed_two = layer_norm(middle, second_gain, second_shift).astype(jnp.bfloat16)
    hidden = jax.nn.gelu(
        jnp.dot(normed_two, expand_matrix, preferred_element_type=jnp.float32)
        + expand_offset.astype(jnp.float32),
        approximate=False,
    ).astype(jnp.bfloat16)
    result = (
        middle.astype(jnp.float32)
        + jnp.dot(hidden, reduce_matrix, preferred_element_type=jnp.float32)
        + shrink_translation.astype(jnp.float32)
    ).astype(jnp.bfloat16)
    return result.reshape(levels, lat_rows, lon_cols, width)


def on_device(
    initial_field,
    first_gain,
    first_shift,
    qkv_weight,
    qkv_bias,
    proj_weight,
    proj_bias,
    second_gain,
    second_shift,
    expand_weight,
    expand_bias,
    reduce_weight,
    reduce_bias,
    earth_bias,
):
    collected_values = (
        lax.all_gather(qkv_weight, "tp", axis=2, tiled=True),
        lax.all_gather(qkv_bias, "tp", axis=1, tiled=True),
        lax.all_gather(proj_weight, "tp", axis=2, tiled=True),
        lax.all_gather(proj_bias, "tp", axis=1, tiled=True),
        lax.all_gather(expand_weight, "tp", axis=2, tiled=True),
        lax.all_gather(expand_bias, "tp", axis=1, tiled=True),
        lax.all_gather(reduce_weight, "tp", axis=1, tiled=True),
        lax.all_gather(reduce_bias, "tp", axis=1, tiled=True),
    )
    weights = tuple((piece[0] for piece in collected_values))
    norms = (first_gain[0], first_shift[0], second_gain[0], second_shift[0])
    bias_table = earth_bias[0, 0, 0]
    table_items = jnp.asarray(bias_entries())
    portion_index = lax.axis_index("section")
    band_half = lax.axis_index("lat") % 2
    micro_count = initial_field.shape[0]
    bias_block = jnp.take(bias_table, table_items, axis=1)
    carried = jnp.zeros_like(initial_field[0])
    daily_lead_times = []
    quarter_lead_times = []
    for turn_index in range(micro_count + 1):
        own_field = initial_field[min(turn_index, micro_count - 1)]
        block_input = jnp.where(portion_index == 0, own_field, carried)
        block_output = earth_block(block_input, norms, weights, bias_block, band_half)
        if turn_index < micro_count:
            daily_lead_times.append(block_output)
            carried = passed_along(block_output, "section", 1)
        if turn_index > 0:
            quarter_lead_times.append(block_output)
    predicted_states = jnp.where(
        portion_index == 0, jnp.stack(daily_lead_times), jnp.stack(quarter_lead_times)
    )
    return predicted_states[None]


def solution(mesh):
    return jax.shard_map(
        on_device,
        mesh=mesh,
        in_specs=(
            P(None, "tp", "lat", None, None),
            P("section", None),
            P("section", None),
            P("section", None, "tp"),
            P("section", "tp"),
            P("section", None, "tp"),
            P("section", "tp"),
            P("section", None),
            P("section", None),
            P("section", None, "tp"),
            P("section", "tp"),
            P("section", "tp", None),
            P("section", "tp"),
            P("section", "tp", "lat", None, None),
        ),
        out_specs=P("section", None, "tp", "lat", None, None),
        check_vma=False,
    )
```

profile of v0, /device:TPU:455, one launch (start us, length us, event | category | flops | bytes accessed | tf_op | source)
XLA Modules:
  0.0 165.5 jit_solution(211439283647402022)
XLA Ops:
  0.0 1.0 convert_reduce_fusion.4
  1.0 1.1 fusion.184
  2.2 0.7 convert_element_type.223
  2.8 0.7 convert_element_type.224
  3.5 1.3 dynamic-slice
  6.7 0.7 reduce.1
  7.4 0.7 reduce.2
  8.1 0.9 dynamic-update-slice.1
  9.0 0.8 dynamic-update-slice.3
  10.3 8.8 %all-reduce.4 = (bf16[768]{0:T(1024)(128)(2,1)S(1)}, bf16[192]{0:T(256)(128)(2,1)S(1)}, bf16[576]{0:T(1024)(128)(2,1)S(1)}, bf16[192]{0:T(256)(128)(2,1)S(1)}) all-reduce(bf16[768]{0:T(1024)(128)(2,1)S(1)} %dynamic-update-slice.2, bf16[192]{0:T(256)(128)(2,1)S(1)} %dynamic-update-slice.1, ...), channel_id=1, replica_groups=mesh['section'=2,'lat'=64,'tp'=4] {'tp'}, use_global_device_ids=true, to_apply=%add.2 | all-reduce | flops 1728 | bytes 6912
  19.1 10.2 %all_gather.24 = bf16[1,192,576]{1,2,0:T(8,128)(2,1)S(1)} all-gather(bf16[1,192,144]{1,2,0:T(8,128)(2,1)} %param.18), channel_id=1, replica_groups=mesh['section'=2,'lat'=64,'tp'=4] {'tp'}, dimensions={2}, use_global_device_ids=true | all-gather | bytes 276480 | tf_op jit(solution)/shard_map/all_gather | solution.py:148
  29.3 1.1 add_convert_fusion.3
  30.9 6.9 %collective-permute-start = (bf16[288,384]{1,0:T(8,128)(2,1)S(1)}, bf16[288,384]{1,0:T(8,128)(2,1)}, u32[]{:S(2)}, u32[]{:S(2)}) collective-permute-start(bf16[288,384]{1,0:T(8,128)(2,1)S(1)} %slice.62), channel_id=1, source_target_pairs={{0,4},{4,0},{8,12},{12,8},{16,20},{20,16},{24,28},{28,24},{32,36},... | collective-permute-start | bytes 663560 | tf_op jit(solution)/shard_map/ppermute | solution.py:20
  38.7 19.9 %gather_fusion = f32[10368,6]{1,0:T(8,128)} fusion(f32[6,1656]{0,1:T(8,128)S(1)} %bitcast.127, s32[11264]{0:T(1024)S(1)} %pad_clamp_fusion), kind=kCustom, calls=%fused_computation | custom fusion | bytes 539136 | tf_op jit(solution)/shard_map/jit(_take)/gather | solution.py:164
  58.6 4.8 %copy.74 = f32[72,144,6]{1,0,2:T(8,128)S(1)} copy(f32[72,144,6]{2,1,0:T(8,128)} %bitcast.128) | data formatting | bytes 497664 | tf_op jit(solution)/shard_map/jit(_take)/gather | solution.py:164
  63.5 9.2 %all_gather.26 = bf16[1,192,192]{1,2,0:T(8,128)(2,1)S(1)} all-gather(bf16[1,192,48]{1,2,0:T(8,128)(2,1)S(1)} %copy-done.10), channel_id=1, replica_groups=mesh['section'=2,'lat'=64,'tp'=4] {'tp'}, dimensions={2}, use_global_device_ids=true | all-gather | bytes 92160 | tf_op jit(solution)/shard_map/all_gather | solution.py:150
  72.7 0.6 add.317
  73.3 0.6 add.318
  74.0 12.2 %all_gather.28 = bf16[1,192,768]{1,0,2:T(2,128)(2,1)S(1)} all-gather(bf16[1,192,192]{1,0,2:T(2,128)(2,1)S(1)} %copy.77), channel_id=1, replica_groups=mesh['section'=2,'lat'=64,'tp'=4] {'tp'}, dimensions={2}, use_global_device_ids=true | all-gather | bytes 368640 | tf_op jit(solution)/shard_map/all_gather | solution.py:152
  86.2 0.5 copy.78
  86.6 10.6 %all_gather.30 = bf16[1,768,192]{2,1,0:T(8,128)(2,1)} all-gather(bf16[1,192,192]{2,1,0:T(8,128)(2,1)} %param.26), channel_id=1, replica_groups=mesh['section'=2,'lat'=64,'tp'=4] {'tp'}, dimensions={1}, use_global_device_ids=true | all-gather | bytes 368640 | tf_op jit(solution)/shard_map/all_gather | solution.py:154
  97.3 1.0 concatenate.51
  99.5 1.1 fusion.354
  100.6 3.8 %fusion.18 = bf16[4,72,6,32]{1,3,2,0:T(8,128)(2,1)} fusion(bf16[4,144,6,32]{1,3,2,0:T(8,128)(2,1)S(1)} %bitcast.155, f32[4,6,72]{2,1,0:T(8,128)S(1)} %fusion.354, f32[6,72,144]{2,1,0:T(8,128)S(1)} %bitcast.143, bf16[4,144,6,32]{1,3,2,0:T(8,128)(2,1)S(1)} %bitcast.151, bf16[4,72,6,32]{3,2,0,1:T(8,128)(2,1)S(1)} %reshape_reshape.9), kind=kOutput, calls=%fused_computation.46 | convolution fusion | flops 33151824 | bytes 919296 | tf_op jit(solution)/shard_map/whqk,wkhd->wqhd/dot_general | solution.py:105
  104.4 1.8 %copy.75 = bf16[4,72,6,32]{3,2,0,1:T(8,128)(2,1)S(1)} copy(bf16[4,72,6,32]{1,3,2,0:T(8,128)(2,1)} %fusion.18) | data formatting | bytes 221184 | tf_op jit(solution)/shard_map/convert_element_type | solution.py:107
  106.3 0.3 reshape.310
  107.3 2.4 %fusion.17 = bf16[288,192]{1,0:T(8,128)(2,1)S(1)} fusion(f32[288,192]{1,0:T(8,128)S(1)} %get-tuple-element.20, f32[768]{0:T(1024)S(1)} %copy-done.11, bf16[1,768,192]{2,1,0:T(8,128)(2,1)S(1)} %copy-done.1, bf16[1,192,768]{2,1,0:T(8,128)(2,1)S(1)} %copy.78, f32[192]{0:T(256)S(1)} %copy-done.22, f32[192]{0:T(256)S(1)} %bitcast.171, f32[192]{0:T(256)S(1)} %bitcast.168, ...), kind=kOutput, calls=%fused_computation.45 | convolution fusion | flops 184909824 | bytes 929280 | tf_op jit(solution)/shard_map/dot_general | solution.py:125
  109.7 1.5 collective-permute-start.1
  111.2 5.9 %collective-permute-done.1 = bf16[2,3,48,192]{3,2,1,0:T(8,128)(2,1)S(1)} collective-permute-done((bf16[2,3,48,192]{3,2,1,0:T(8,128)(2,1)S(1)}, bf16[2,3,48,192]{3,2,1,0:T(8,128)(2,1)S(1)}, u32[]{:S(2)}, u32[]{:S(2)}) %collective-permute-start.1) | collective-permute-done | bytes 110624 | tf_op jit(solution)/shard_map/ppermute | solution.py:26
  118.1 10.0 %collective-permute-start.2 = (bf16[288,384]{1,0:T(8,128)(2,1)S(1)}, bf16[288,384]{1,0:T(8,128)(2,1)S(1)}, u32[]{:S(2)}, u32[]{:S(2)}) collective-permute-start(bf16[288,384]{1,0:T(8,128)(2,1)S(1)} %slice.66), channel_id=1, source_target_pairs={{0,4},{4,0},{8,12},{12,8},{16,20},{20,16},{24,28},{28,24},{32,36},... | collective-permute-start | bytes 663560 | tf_op jit(solution)/shard_map/ppermute | solution.py:20
  128.6 0.6 collective-permute-done.2
  130.2 1.0 copy.80
  131.2 1.7 %fusion.358 = f32[4,6,72]{2,1,0:T(8,128)} fusion(f32[6,72,144]{2,1,0:T(8,128)S(1)} %bitcast.144, bf16[4,144,6,32]{1,3,2,0:T(8,128)(2,1)S(1)} %bitcast.152, bf16[4,72,6,32]{3,2,0,1:T(8,128)(2,1)S(1)} %reshape_reshape.10), kind=kOutput, calls=%fused_computation.393 | convolution fusion | flops 16920720 | bytes 587520 | tf_op jit(solution)/shard_map/sub | solution.py:104
  132.9 3.9 %fusion.19 = bf16[4,72,6,32]{1,3,2,0:T(8,128)(2,1)S(1)} fusion(bf16[4,144,6,32]{1,3,2,0:T(8,128)(2,1)S(1)} %bitcast.156, f32[4,6,72]{2,1,0:T(8,128)} %fusion.358, f32[6,72,144]{2,1,0:T(8,128)S(1)} %bitcast.145, bf16[4,144,6,32]{1,3,2,0:T(8,128)(2,1)S(1)} %bitcast.153, bf16[4,72,6,32]{3,2,0,1:T(8,128)(2,1)S(1)} %reshape_reshape.10), kind=kOutput, calls=%fused_computation.47 | convolution fusion | flops 33151824 | bytes 919296 | tf_op jit(solution)/shard_map/whqk,wkhd->wqhd/dot_general | solution.py:105
  136.8 0.9 copy.84
  137.7 0.3 reshape.318
  138.8 2.4 %fusion.16 = bf16[288,192]{1,0:T(8,128)(2,1)S(1)} fusion(f32[768]{0:T(1024)S(1)} %copy-done.12, bf16[288,192]{1,0:T(8,128)(2,1)S(1)} %fusion.189, bf16[1,768,192]{2,1,0:T(8,128)(2,1)S(1)} %copy-done.1, bf16[1,192,768]{2,1,0:T(8,128)(2,1)S(1)} %copy.78, f32[192]{0:T(256)S(1)} %copy-done.23, f32[288]{0:T(512)S(1)} %add_rsqrt_fusion.4, ...), kind=kOutput, calls=%fused_computation.44 | convolution fusion | flops 185020416 | bytes 818688 | tf_op jit(solution)/shard_map/dot_general | solution.py:125
  141.2 1.3 collective-permute-start.3
  142.5 7.2 %collective-permute-done.3 = bf16[2,3,48,192]{3,2,1,0:T(8,128)(2,1)S(1)} collective-permute-done((bf16[2,3,48,192]{3,2,1,0:T(8,128)(2,1)S(1)}, bf16[2,3,48,192]{3,2,1,0:T(8,128)(2,1)S(1)}, u32[]{:S(2)}, u32[]{:S(2)}) %collective-permute-start.3) | collective-permute-done | bytes 110624 | tf_op jit(solution)/shard_map/ppermute | solution.py:26
  150.1 0.3 fusion.8
  150.6 3.3 %collective-permute-start.4 = (bf16[288,384]{1,0:T(8,128)(2,1)S(1)}, bf16[288,384]{1,0:T(8,128)(2,1)S(1)}, u32[]{:S(2)}, u32[]{:S(2)}) collective-permute-start(bf16[288,384]{1,0:T(8,128)(2,1)S(1)} %slice.70), channel_id=1, source_target_pairs={{0,4},{4,0},{8,12},{12,8},{16,20},{20,16},{24,28},{28,24},{32,36},... | collective-permute-start | bytes 663560 | tf_op jit(solution)/shard_map/ppermute | solution.py:20
  154.4 0.4 collective-permute-done.4
  156.0 1.1 fusion.361
  157.1 3.1 %fusion.20 = bf16[4,72,6,32]{1,3,2,0:T(8,128)(2,1)S(1)} fusion(bf16[4,144,6,32]{1,3,2,0:T(8,128)(2,1)S(1)} %bitcast.154, f32[4,6,72]{2,1,0:T(8,128)S(1)} %fusion.361, f32[6,72,144]{2,1,0:T(8,128)S(1)} %bitcast.147, bf16[4,144,6,32]{1,3,2,0:T(8,128)(2,1)S(1)} %bitcast.149, bf16[4,72,6,32]{3,2,0,1:T(8,128)(2,1)S(1)} %reshape_reshape.11), kind=kOutput, calls=%fused_computation.48 | convolution fusion | flops 33151824 | bytes 919296 | tf_op jit(solution)/shard_map/whqk,wkhd->wqhd/dot_general | solution.py:105
  160.3 0.9 copy.91
  161.2 0.3 reshape.326
  162.3 2.4 %fusion.15 = bf16[288,192]{1,0:T(8,128)(2,1)S(1)} fusion(f32[768]{0:T(1024)S(1)} %copy-done.13, bf16[288,192]{1,0:T(8,128)(2,1)S(1)} %fusion.190, bf16[1,768,192]{2,1,0:T(8,128)(2,1)S(1)} %copy-done.1, bf16[1,192,768]{2,1,0:T(8,128)(2,1)S(1)} %copy.78, f32[192]{0:T(256)S(1)} %copy-done.24, f32[288]{0:T(512)S(1)} %add_rsqrt_fusion.3, ...), kind=kOutput, calls=%fused_computation.43 | convolution fusion | flops 185020416 | bytes 818688 | tf_op jit(solution)/shard_map/dot_general | solution.py:125
  164.7 0.8 maximum_select_fusion.3
  (133 shorter events, 9.8 us)
Async XLA Ops:
  30.4 7.9 %copy-start.9 = (f32[1,1,1,6,1656]{4,2,3,1,0:T(1,128)S(1)}, f32[1,1,1,6,1656]{4,2,3,1,0:T(1,128)}, u32[]{:S(2)}) copy-start(f32[1,1,1,6,1656]{4,2,3,1,0:T(1,128)} %param.28) | copy-start | bytes 119236
  30.7 7.9 %copy-start.8 = (s32[10368]{0:T(1024)S(1)}, s32[10368]{0:T(1024)}, u32[]{:S(2)}) copy-start(s32[10368]{0:T(1024)} %constant.152) | copy-start | bytes 124420
  30.9 66.4 %collective-permute-start = (bf16[288,384]{1,0:T(8,128)(2,1)S(1)}, bf16[288,384]{1,0:T(8,128)(2,1)}, u32[]{:S(2)}, u32[]{:S(2)}) collective-permute-start(bf16[288,384]{1,0:T(8,128)(2,1)S(1)} %slice.62), channel_id=1, source_target_pairs={{0,4},{4,0},{8,12},{12,8},{16,20},{20,16},{24,28},{28,24},{32,36},... | collective-permute-start | bytes 663560 | tf_op jit(solution)/shard_map/ppermute | solution.py:20
  58.6 4.9 %copy-start.10 = (bf16[1,192,48]{1,2,0:T(8,128)(2,1)S(1)}, bf16[1,192,48]{1,2,0:T(8,128)(2,1)}, u32[]{:S(2)}) copy-start(bf16[1,192,48]{1,2,0:T(8,128)(2,1)} %param.20) | copy-start | bytes 55300
  58.6 15.2 %copy-start.7 = (bf16[1,192,192]{2,1,0:T(8,128)(2,1)S(1)}, bf16[1,192,192]{2,1,0:T(8,128)(2,1)}, u32[]{:S(2)}) copy-start(bf16[1,192,192]{2,1,0:T(8,128)(2,1)} %param.24) | copy-start | bytes 221188
  63.4 33.8 %copy-start.14 = (bf16[1,192]{1,0:T(2,128)(2,1)S(1)}, bf16[1,192]{1,0:T(2,128)(2,1)}, u32[]{:S(2)}) copy-start(bf16[1,192]{1,0:T(2,128)(2,1)} %param.22) | copy-start | bytes 1156
  63.4 33.8 %copy-start.15 = (bf16[1,192]{1,0:T(2,128)(2,1)S(1)}, bf16[1,192]{1,0:T(2,128)(2,1)}, u32[]{:S(2)}) copy-start(bf16[1,192]{1,0:T(2,128)(2,1)} %param.23) | copy-start | bytes 1156
  63.5 33.8 %copy-start = (bf16[2,2,3,48,192]{4,3,2,1,0:T(8,128)(2,1)S(1)}, bf16[2,2,3,48,192]{4,3,2,1,0:T(8,128)(2,1)}, u32[]{:S(2)}) copy-start(bf16[2,2,3,48,192]{4,3,2,1,0:T(8,128)(2,1)} %param.15) | copy-start | bytes 663556
  97.2 10.0 %copy-start.16 = (f32[1,192]{1,0:T(1,128)}, f32[1,192]{1,0:T(1,128)S(1)}, u32[]{:S(2)}) copy-start(f32[1,192]{1,0:T(1,128)S(1)} %mul.170) | copy-start | bytes 2308
  97.3 10.0 %copy-start.19 = (f32[1,192]{1,0:T(1,128)}, f32[1,192]{1,0:T(1,128)S(1)}, u32[]{:S(2)}) copy-start(f32[1,192]{1,0:T(1,128)S(1)} %add.304) | copy-start | bytes 2308
  104.4 2.9 %copy-start.1 = (bf16[1,768,192]{2,1,0:T(8,128)(2,1)S(1)}, bf16[1,768,192]{2,1,0:T(8,128)(2,1)}, u32[]{:S(2)}) copy-start(bf16[1,768,192]{2,1,0:T(8,128)(2,1)} %all_gather.30) | copy-start | bytes 884740
  104.4 2.9 %copy-start.11 = (f32[768]{0:T(1024)S(1)}, f32[768]{0:T(1024)}, u32[]{:S(2)}) copy-start(f32[768]{0:T(1024)} %add.317) | copy-start | bytes 9220
  104.4 2.9 %copy-start.22 = (f32[192]{0:T(256)S(1)}, f32[192]{0:T(256)}, u32[]{:S(2)}) copy-start(f32[192]{0:T(256)} %add.318) | copy-start | bytes 2308
  109.7 7.9 %copy-start.3 = (bf16[288,192]{1,0:T(8,128)(2,1)}, bf16[288,192]{1,0:T(8,128)(2,1)S(1)}, u32[]{:S(2)}) copy-start(bf16[288,192]{1,0:T(8,128)(2,1)S(1)} %fusion.17) | copy-start | bytes 331780
  109.7 7.4 %collective-permute-start.1 = (bf16[2,3,48,192]{3,2,1,0:T(8,128)(2,1)S(1)}, bf16[2,3,48,192]{3,2,1,0:T(8,128)(2,1)S(1)}, u32[]{:S(2)}, u32[]{:S(2)}) collective-permute-start(bf16[2,3,48,192]{3,2,1,0:T(8,128)(2,1)S(1)} %bitcast.157), channel_id=1, source_target_pairs={{0,256},{1,257},{2,258},{3,259},{4,260},{5,261},{6,262},{7,263},{8... | collective-permute-start | bytes 331784 | tf_op jit(solution)/shard_map/ppermute | solution.py:26
  118.1 11.1 %collective-permute-start.2 = (bf16[288,384]{1,0:T(8,128)(2,1)S(1)}, bf16[288,384]{1,0:T(8,128)(2,1)S(1)}, u32[]{:S(2)}, u32[]{:S(2)}) collective-permute-start(bf16[288,384]{1,0:T(8,128)(2,1)S(1)} %slice.66), channel_id=1, source_target_pairs={{0,4},{4,0},{8,12},{12,8},{16,20},{20,16},{24,28},{28,24},{32,36},... | collective-permute-start | bytes 663560 | tf_op jit(solution)/shard_map/ppermute | solution.py:20
  131.2 1.7 %copy-start.2 = (bf16[4,144,192]{1,2,0:T(8,128)(2,1)S(1)}, bf16[4,144,192]{1,2,0:T(8,128)(2,1)}, u32[]{:S(2)}) copy-start(bf16[4,144,192]{1,2,0:T(8,128)(2,1)} %copy.80) | copy-start | bytes 663556
  136.8 2.0 %copy-start.12 = (f32[768]{0:T(1024)S(1)}, f32[768]{0:T(1024)}, u32[]{:S(2)}) copy-start(f32[768]{0:T(1024)} %add.317) | copy-start | bytes 9220
  136.8 2.0 %copy-start.17 = (f32[1,192]{1,0:T(1,128)S(1)}, f32[1,192]{1,0:T(1,128)}, u32[]{:S(2)}) copy-start(f32[1,192]{1,0:T(1,128)} %copy-done.16) | copy-start | bytes 2308
  136.8 2.0 %copy-start.20 = (f32[1,192]{1,0:T(1,128)S(1)}, f32[1,192]{1,0:T(1,128)}, u32[]{:S(2)}) copy-start(f32[1,192]{1,0:T(1,128)} %copy-done.19) | copy-start | bytes 2308
  136.8 2.0 %copy-start.23 = (f32[192]{0:T(256)S(1)}, f32[192]{0:T(256)}, u32[]{:S(2)}) copy-start(f32[192]{0:T(256)} %add.318) | copy-start | bytes 2308
  141.2 1.3 copy-start.5
  141.2 8.5 %collective-permute-start.3 = (bf16[2,3,48,192]{3,2,1,0:T(8,128)(2,1)S(1)}, bf16[2,3,48,192]{3,2,1,0:T(8,128)(2,1)S(1)}, u32[]{:S(2)}, u32[]{:S(2)}) collective-permute-start(bf16[2,3,48,192]{3,2,1,0:T(8,128)(2,1)S(1)} %bitcast.159), channel_id=1, source_target_pairs={{0,256},{1,257},{2,258},{3,259},{4,260},{5,261},{6,262},{7,263},{8... | collective-permute-start | bytes 331784 | tf_op jit(solution)/shard_map/ppermute | solution.py:26
  150.6 4.2 %collective-permute-start.4 = (bf16[288,384]{1,0:T(8,128)(2,1)S(1)}, bf16[288,384]{1,0:T(8,128)(2,1)S(1)}, u32[]{:S(2)}, u32[]{:S(2)}) collective-permute-start(bf16[288,384]{1,0:T(8,128)(2,1)S(1)} %slice.70), channel_id=1, source_target_pairs={{0,4},{4,0},{8,12},{12,8},{16,20},{20,16},{24,28},{28,24},{32,36},... | collective-permute-start | bytes 663560 | tf_op jit(solution)/shard_map/ppermute | solution.py:20
  160.3 2.0 %copy-start.13 = (f32[768]{0:T(1024)S(1)}, f32[768]{0:T(1024)}, u32[]{:S(2)}) copy-start(f32[768]{0:T(1024)} %add.317) | copy-start | bytes 9220
  160.3 2.0 %copy-start.18 = (f32[1,192]{1,0:T(1,128)S(1)}, f32[1,192]{1,0:T(1,128)}, u32[]{:S(2)}) copy-start(f32[1,192]{1,0:T(1,128)} %copy-done.16) | copy-start | bytes 2308
  160.3 2.0 %copy-start.21 = (f32[1,192]{1,0:T(1,128)S(1)}, f32[1,192]{1,0:T(1,128)}, u32[]{:S(2)}) copy-start(f32[1,192]{1,0:T(1,128)} %copy-done.19) | copy-start | bytes 2308
  160.3 2.0 %copy-start.24 = (f32[192]{0:T(256)S(1)}, f32[192]{0:T(256)}, u32[]{:S(2)}) copy-start(f32[192]{0:T(256)} %add.318) | copy-start | bytes 2308
  162.3 2.4 %copy-start.4 = (bf16[288,192]{1,0:T(8,128)(2,1)S(1)}, bf16[288,192]{1,0:T(8,128)(2,1)}, u32[]{:S(2)}) copy-start(bf16[288,192]{1,0:T(8,128)(2,1)} %copy-done.3) | copy-start | bytes 331780
  162.3 2.4 %copy-start.6 = (bf16[288,192]{1,0:T(8,128)(2,1)S(1)}, bf16[288,192]{1,0:T(8,128)(2,1)}, u32[]{:S(2)}) copy-start(bf16[288,192]{1,0:T(8,128)(2,1)} %copy-done.5) | copy-start | bytes 331780
where the time goes:
time: 166 us
  blocking collectives  50.9 us (31%)
  local copies, waits for them, and re-layouts  40.5 us (24%)
  matrix products  23.5 us (14%)
  starting transfers between devices  23 us (14%)
  waiting for transfers between devices  14 us (8%)
  other arithmetic  10.6 us (6%)
  between operations  2.91 us (2%)
    gather x2, local copies, waits for them, and re-layouts, on_device(): bias_block = jnp.take(bias_table, table_items, axis=1)  24.8 us
    ppermute x3, starting transfers between devices, swapped(): return lax.ppermute(block, axis, route)  20.3 us
    ppermute x2, waiting for transfers between devices, passed_along(): lax.ppermute(value, axis, [(source, source + steps) for source in range(f...  13.1 us
    all_gather x1, blocking collectives, on_device(): lax.all_gather(expand_weight, 'tp', axis=2, tiled=True)  12.2 us
    dot_general x3, matrix products, earth_block(): jnp.einsum('whqk,wkhd->wqhd', probs, value_heads, preferred_element_type=...  10.8 us
    all_gather x1, blocking collectives, on_device(): lax.all_gather(reduce_weight, 'tp', axis=1, tiled=True)  10.6 us
    all_gather x1, blocking collectives, on_device(): lax.all_gather(qkv_weight, 'tp', axis=2, tiled=True)  10.2 us
    all_gather x1, blocking collectives, on_device(): lax.all_gather(proj_weight, 'tp', axis=2, tiled=True)  9.17 us
  transfers between devices with their start and end apart: 5, of which 4 were waited for; matrix products, arithmetic and copies ran while one was open for 17% of the time, Pallas kernels for 0%

commit v1 on v0

--- a/solution.py
+++ b/solution.py
@@ -145,7 +145,9 @@
     earth_bias,
 ):
     collected_values = (
-        lax.all_gather(qkv_weight, "tp", axis=2, tiled=True),
+        jnp.concatenate(
+            lax.all_to_all(jnp.stack([qkv_weight] * lax.axis_size("tp")), "tp", 0, 0), axis=2
+        ),
         lax.all_gather(qkv_bias, "tp", axis=1, tiled=True),
         lax.all_gather(proj_weight, "tp", axis=2, tiled=True),
         lax.all_gather(proj_bias, "tp", axis=1, tiled=True),

time: 166 us -> 159 us (0.958)
  the two profiles are of different devices: /device:TPU:455 before, /device:TPU:5 now
where the time goes in v1:
time: 159 us; the launch traced here: 158 us
  local copies, waits for them, and re-layouts  42.6 us (27%)
  blocking collectives  39.2 us (25%)
  starting transfers between devices  27.7 us (17%)
  matrix products  21.6 us (14%)
  waiting for transfers between devices  15.9 us (10%)
  other arithmetic  7.95 us (5%)
  between operations  2.95 us (2%)
    gather x2, local copies, waits for them, and re-layouts, on_device(): bias_block = jnp.take(bias_table, table_items, axis=1)  24.8 us
    ppermute x3, starting transfers between devices, swapped(): return lax.ppermute(block, axis, route)  20.9 us
    ppermute x2, waiting for transfers between devices, passed_along(): lax.ppermute(value, axis, [(source, source + steps) for source in range(f...  14.6 us
    all_gather x1, blocking collectives, on_device(): lax.all_gather(expand_weight, 'tp', axis=2, tiled=True)  12.8 us
    all_gather x1, blocking collectives, on_device(): lax.all_gather(reduce_weight, 'tp', axis=1, tiled=True)  10.7 us
    dot_general x3, matrix products, earth_block(): jnp.einsum('whqk,wkhd->wqhd', probs, value_heads, preferred_element_type=...  9.46 us
    all_gather x1, blocking collectives, on_device(): lax.all_gather(proj_weight, 'tp', axis=2, tiled=True)  9.04 us
    dot_general x3, matrix products, earth_block(): jnp.dot(hidden, reduce_matrix, preferred_element_type=jnp.float32)  7.16 us
  transfers between devices with their start and end apart: 6, of which 5 were waited for; matrix products, arithmetic and copies ran while one was open for 22% of the time, Pallas kernels for 0%

profile of v1, /device:TPU:5, one launch (start us, length us, event | category | flops | bytes accessed | tf_op | source)
XLA Modules:
  0.0 157.9 jit_solution(10608782921253514263)
XLA Ops:
  0.0 1.7 %stack.19 = bf16[4,1,192,144]{2,3,1,0:T(8,128)(2,1)} broadcast(bf16[192,144]{0,1:T(8,128)(2,1)} %bitcast.165), dimensions={2,3} | broadcast | bytes 276480 | tf_op jit(solution)/shard_map/stack | solution.py:149
  1.7 4.2 %all-to-all-start = ((bf16[4,1,192,144]{2,3,1,0:T(8,128)(2,1)}), bf16[4,1,192,144]{2,3,1,0:T(8,128)(2,1)S(1)}, u32[]{:S(2)}, u32[]{:S(2)}) async-start(bf16[4,1,192,144]{2,3,1,0:T(8,128)(2,1)} %stack.19), calls=%async_computation | async-start | bytes 589824 | tf_op jit(solution)/shard_map/all_to_all | solution.py:149
  5.9 1.0 convert_reduce_fusion.4
  6.9 1.1 fusion.181
  8.0 0.7 convert_element_type.223
  8.7 0.7 convert_element_type.224
  9.4 0.8 pad_clamp_fusion
  10.2 1.1 copy.78
  11.4 12.8 %all_gather.24 = bf16[1,192,768]{1,0,2:T(2,128)(2,1)S(1)} all-gather(bf16[1,192,192]{1,0,2:T(2,128)(2,1)S(1)} %copy.78), channel_id=1, replica_groups=mesh['section'=2,'lat'=64,'tp'=4] {'tp'}, dimensions={2}, use_global_device_ids=true | all-gather | bytes 368640 | tf_op jit(solution)/shard_map/all_gather | solution.py:154
  24.2 1.3 dynamic-slice
  28.4 6.7 %all-reduce.4 = (bf16[768]{0:T(1024)(128)(2,1)S(1)}, bf16[192]{0:T(256)(128)(2,1)S(1)}, bf16[576]{0:T(1024)(128)(2,1)S(1)}, bf16[192]{0:T(256)(128)(2,1)S(1)}) all-reduce(bf16[768]{0:T(1024)(128)(2,1)S(1)} %dynamic-update-slice.2, bf16[192]{0:T(256)(128)(2,1)S(1)} %dynamic-update-slice.1, ...), channel_id=1, replica_groups=mesh['section'=2,'lat'=64,'tp'=4] {'tp'}, use_global_device_ids=true, to_apply=%add.2 | all-reduce | flops 1728 | bytes 6912
  35.1 0.3 copy.74
  35.5 19.9 %gather_fusion = f32[10368,6]{1,0:T(8,128)} fusion(f32[6,1656]{0,1:T(8,128)S(1)} %bitcast.127, s32[11264]{0:T(1024)S(1)} %pad_clamp_fusion), kind=kCustom, calls=%fused_computation | custom fusion | bytes 539136 | tf_op jit(solution)/shard_map/jit(_take)/gather | solution.py:166
  55.4 4.8 %copy.75 = f32[72,144,6]{1,0,2:T(8,128)S(1)} copy(f32[72,144,6]{2,1,0:T(8,128)} %bitcast.128) | data formatting | bytes 497664 | tf_op jit(solution)/shard_map/jit(_take)/gather | solution.py:166
  60.3 0.5 copy.79
  60.9 9.0 %all_gather.22 = bf16[1,192,192]{1,2,0:T(8,128)(2,1)S(1)} all-gather(bf16[1,192,48]{1,2,0:T(8,128)(2,1)S(1)} %copy-done.11), channel_id=1, replica_groups=mesh['section'=2,'lat'=64,'tp'=4] {'tp'}, dimensions={2}, use_global_device_ids=true | all-gather | bytes 92160 | tf_op jit(solution)/shard_map/all_gather | solution.py:152
  69.9 10.7 %all_gather.26 = bf16[1,768,192]{2,1,0:T(8,128)(2,1)} all-gather(bf16[1,192,192]{2,1,0:T(8,128)(2,1)S(1)} %copy-done.9), channel_id=1, replica_groups=mesh['section'=2,'lat'=64,'tp'=4] {'tp'}, dimensions={1}, use_global_device_ids=true | all-gather | bytes 368640 | tf_op jit(solution)/shard_map/all_gather | solution.py:156
  81.1 14.4 %collective-permute-start = (bf16[288,384]{1,0:T(8,128)(2,1)S(1)}, bf16[288,384]{1,0:T(8,128)(2,1)}, u32[]{:S(2)}, u32[]{:S(2)}) collective-permute-start(bf16[288,384]{1,0:T(8,128)(2,1)S(1)} %slice.62), channel_id=1, source_target_pairs={{0,4},{4,0},{8,12},{12,8},{16,20},{20,16},{24,28},{28,24},{32,36},... | collective-permute-start | bytes 663560 | tf_op jit(solution)/shard_map/ppermute | solution.py:20
  96.0 0.5 collective-permute-done
  96.5 1.0 concatenate.51
  98.4 1.0 copy.70
  99.4 1.1 fusion.351
  100.5 3.1 %fusion.18 = bf16[4,72,6,32]{1,3,2,0:T(8,128)(2,1)S(1)} fusion(bf16[4,144,6,32]{1,3,2,0:T(8,128)(2,1)S(1)} %bitcast.158, f32[4,6,72]{2,1,0:T(8,128)S(1)} %fusion.351, f32[6,72,144]{2,1,0:T(8,128)S(1)} %bitcast.146, bf16[4,144,6,32]{1,3,2,0:T(8,128)(2,1)S(1)} %bitcast.154, bf16[4,72,6,32]{3,2,0,1:T(8,128)(2,1)S(1)} %reshape_reshape.9), kind=kOutput, calls=%fused_computation.46 | convolution fusion | flops 33151824 | bytes 919296 | tf_op jit(solution)/shard_map/whqk,wkhd->wqhd/dot_general | solution.py:105
  103.7 0.8 copy.76
  104.5 0.3 reshape.317
  105.0 0.3 fusion.354
  105.6 2.4 %fusion.17 = bf16[288,192]{1,0:T(8,128)(2,1)S(1)} fusion(f32[288,192]{1,0:T(8,128)S(1)} %get-tuple-element.20, f32[768]{0:T(1024)S(1)} %add.317, bf16[1,768,192]{2,1,0:T(8,128)(2,1)S(1)} %copy-done.1, bf16[1,192,768]{2,1,0:T(8,128)(2,1)S(1)} %copy.79, f32[192]{0:T(256)S(1)} %add.318, f32[192]{0:T(256)S(1)} %bitcast.175, f32[192]{0:T(256)S(1)} %bitcast.172, ...), kind=kOutput, calls=%fused_computation.45 | convolution fusion | flops 184909824 | bytes 929280 | tf_op jit(solution)/shard_map/dot_general | solution.py:125
  108.0 1.3 collective-permute-start.1
  109.3 7.5 %collective-permute-done.1 = bf16[2,3,48,192]{3,2,1,0:T(8,128)(2,1)S(1)} collective-permute-done((bf16[2,3,48,192]{3,2,1,0:T(8,128)(2,1)S(1)}, bf16[2,3,48,192]{3,2,1,0:T(8,128)(2,1)S(1)}, u32[]{:S(2)}, u32[]{:S(2)}) %collective-permute-start.1) | collective-permute-done | bytes 110624 | tf_op jit(solution)/shard_map/ppermute | solution.py:26
  117.3 0.3 fusion.7
  117.7 3.2 %collective-permute-start.2 = (bf16[288,384]{1,0:T(8,128)(2,1)S(1)}, bf16[288,384]{1,0:T(8,128)(2,1)}, u32[]{:S(2)}, u32[]{:S(2)}) collective-permute-start(bf16[288,384]{1,0:T(8,128)(2,1)S(1)} %slice.66), channel_id=1, source_target_pairs={{0,4},{4,0},{8,12},{12,8},{16,20},{20,16},{24,28},{28,24},{32,36},... | collective-permute-start | bytes 663560 | tf_op jit(solution)/shard_map/ppermute | solution.py:20
  121.4 0.5 collective-permute-done.2
  121.9 1.0 concatenate.55
  124.1 1.1 fusion.355
  125.2 3.2 %fusion.19 = bf16[4,72,6,32]{1,3,2,0:T(8,128)(2,1)S(1)} fusion(bf16[4,144,6,32]{1,3,2,0:T(8,128)(2,1)S(1)} %bitcast.159, f32[4,6,72]{2,1,0:T(8,128)S(1)} %fusion.355, f32[6,72,144]{2,1,0:T(8,128)S(1)} %bitcast.148, bf16[4,144,6,32]{1,3,2,0:T(8,128)(2,1)S(1)} %bitcast.156, bf16[4,72,6,32]{3,2,0,1:T(8,128)(2,1)S(1)} %reshape_reshape.10), kind=kOutput, calls=%fused_computation.47 | convolution fusion | flops 33151824 | bytes 919296 | tf_op jit(solution)/shard_map/whqk,wkhd->wqhd/dot_general | solution.py:105
  128.4 0.8 copy.85
  129.2 0.3 reshape.325
  130.3 2.4 %fusion.16 = bf16[288,192]{1,0:T(8,128)(2,1)S(1)} fusion(f32[768]{0:T(1024)S(1)} %add.317, bf16[288,192]{1,0:T(8,128)(2,1)S(1)} %fusion.186, bf16[1,768,192]{2,1,0:T(8,128)(2,1)S(1)} %copy-done.2, bf16[1,192,768]{2,1,0:T(8,128)(2,1)S(1)} %copy.79, f32[192]{0:T(256)S(1)} %add.318, f32[288]{0:T(512)S(1)} %add_rsqrt_fusion.4, ...), kind=kOutput, calls=%fused_computation.44 | convolution fusion | flops 185020416 | bytes 818688 | tf_op jit(solution)/shard_map/dot_general | solution.py:125
  132.7 1.3 collective-permute-start.3
  134.0 7.2 %collective-permute-done.3 = bf16[2,3,48,192]{3,2,1,0:T(8,128)(2,1)S(1)} collective-permute-done((bf16[2,3,48,192]{3,2,1,0:T(8,128)(2,1)S(1)}, bf16[2,3,48,192]{3,2,1,0:T(8,128)(2,1)S(1)}, u32[]{:S(2)}, u32[]{:S(2)}) %collective-permute-start.3) | collective-permute-done | bytes 110624 | tf_op jit(solution)/shard_map/ppermute | solution.py:26
  142.2 3.4 %collective-permute-start.4 = (bf16[288,384]{1,0:T(8,128)(2,1)S(1)}, bf16[288,384]{1,0:T(8,128)(2,1)S(1)}, u32[]{:S(2)}, u32[]{:S(2)}) collective-permute-start(bf16[288,384]{1,0:T(8,128)(2,1)S(1)} %slice.70), channel_id=1, source_target_pairs={{0,4},{4,0},{8,12},{12,8},{16,20},{20,16},{24,28},{28,24},{32,36},... | collective-permute-start | bytes 663560 | tf_op jit(solution)/shard_map/ppermute | solution.py:20
  147.4 1.0 copy.88
  148.4 1.1 fusion.358
  149.5 3.2 %fusion.20 = bf16[4,72,6,32]{1,3,2,0:T(8,128)(2,1)S(1)} fusion(bf16[4,144,6,32]{1,3,2,0:T(8,128)(2,1)S(1)} %bitcast.157, f32[4,6,72]{2,1,0:T(8,128)S(1)} %fusion.358, f32[6,72,144]{2,1,0:T(8,128)S(1)} %bitcast.150, bf16[4,144,6,32]{1,3,2,0:T(8,128)(2,1)S(1)} %bitcast.152, bf16[4,72,6,32]{3,2,0,1:T(8,128)(2,1)S(1)} %reshape_reshape.11), kind=kOutput, calls=%fused_computation.48 | convolution fusion | flops 33151824 | bytes 919296 | tf_op jit(solution)/shard_map/whqk,wkhd->wqhd/dot_general | solution.py:105
  152.7 0.9 copy.92
  153.6 0.3 reshape.333
  154.7 2.4 %fusion.15 = bf16[288,192]{1,0:T(8,128)(2,1)S(1)} fusion(f32[768]{0:T(1024)S(1)} %copy-done.19, bf16[288,192]{1,0:T(8,128)(2,1)S(1)} %fusion.187, bf16[1,768,192]{2,1,0:T(8,128)(2,1)S(1)} %copy-done.2, bf16[1,192,768]{2,1,0:T(8,128)(2,1)S(1)} %copy.79, f32[192]{0:T(256)S(1)} %copy-done.31, f32[288]{0:T(512)S(1)} %add_rsqrt_fusion.3, ...), kind=kOutput, calls=%fused_computation.43 | convolution fusion | flops 185020416 | bytes 818688 | tf_op jit(solution)/shard_map/dot_general | solution.py:125
  157.1 0.8 maximum_select_fusion.3
  (149 shorter events, 9.7 us)
Async XLA Ops:
  0.0 11.3 %copy-start = (bf16[2,2,3,48,192]{4,3,2,1,0:T(8,128)(2,1)S(1)}, bf16[2,2,3,48,192]{4,3,2,1,0:T(8,128)(2,1)}, u32[]{:S(2)}) copy-start(bf16[2,2,3,48,192]{4,3,2,1,0:T(8,128)(2,1)} %param.15) | copy-start | bytes 663556
  0.0 27.4 %copy-start.20 = (bf16[1,144]{1,0:T(2,128)(2,1)S(1)}, bf16[1,144]{1,0:T(2,128)(2,1)}, u32[]{:S(2)}) copy-start(bf16[1,144]{1,0:T(2,128)(2,1)} %param.19) | copy-start | bytes 868
  0.0 27.4 %copy-start.21 = (bf16[1,192]{1,0:T(2,128)(2,1)S(1)}, bf16[1,192]{1,0:T(2,128)(2,1)}, u32[]{:S(2)}) copy-start(bf16[1,192]{1,0:T(2,128)(2,1)} %param.25) | copy-start | bytes 1156
  0.0 27.5 %copy-start.28 = (bf16[1,48]{1,0:T(2,128)(2,1)S(1)}, bf16[1,48]{1,0:T(2,128)(2,1)}, u32[]{:S(2)}) copy-start(bf16[1,48]{1,0:T(2,128)(2,1)} %param.21) | copy-start | bytes 292
  0.0 27.7 %copy-start.29 = (bf16[1,48]{1,0:T(2,128)(2,1)S(1)}, bf16[1,48]{1,0:T(2,128)(2,1)}, u32[]{:S(2)}) copy-start(bf16[1,48]{1,0:T(2,128)(2,1)} %param.27) | copy-start | bytes 292
  0.0 35.1 %copy-start.10 = (f32[1,1,1,6,1656]{4,2,3,1,0:T(1,128)S(1)}, f32[1,1,1,6,1656]{4,2,3,1,0:T(1,128)}, u32[]{:S(2)}) copy-start(f32[1,1,1,6,1656]{4,2,3,1,0:T(1,128)} %param.28) | copy-start | bytes 119236
  1.7 78.9 %all-to-all-start = ((bf16[4,1,192,144]{2,3,1,0:T(8,128)(2,1)}), bf16[4,1,192,144]{2,3,1,0:T(8,128)(2,1)S(1)}, u32[]{:S(2)}, u32[]{:S(2)}) async-start(bf16[4,1,192,144]{2,3,1,0:T(8,128)(2,1)} %stack.19), calls=%async_computation | async-start | bytes 589824 | tf_op jit(solution)/shard_map/all_to_all | solution.py:149
  8.7 26.4 %copy-start.12 = (f32[1,192]{1,0:T(1,128)}, f32[1,192]{1,0:T(1,128)S(1)}, u32[]{:S(2)}) copy-start(f32[1,192]{1,0:T(1,128)S(1)} %convert_element_type.223) | copy-start | bytes 2308
  9.4 25.7 %copy-start.14 = (f32[1,192]{1,0:T(1,128)}, f32[1,192]{1,0:T(1,128)S(1)}, u32[]{:S(2)}) copy-start(f32[1,192]{1,0:T(1,128)S(1)} %convert_element_type.224) | copy-start | bytes 2308
  55.4 5.4 %copy-start.22 = (bf16[1,192]{1,0:T(2,128)(2,1)S(1)}, bf16[1,192]{1,0:T(2,128)(2,1)}, u32[]{:S(2)}) copy-start(bf16[1,192]{1,0:T(2,128)(2,1)} %param.22) | copy-start | bytes 1156
  55.4 5.4 %copy-start.23 = (bf16[1,192]{1,0:T(2,128)(2,1)S(1)}, bf16[1,192]{1,0:T(2,128)(2,1)}, u32[]{:S(2)}) copy-start(bf16[1,192]{1,0:T(2,128)(2,1)} %param.23) | copy-start | bytes 1156
  55.4 5.5 %copy-start.11 = (bf16[1,192,48]{1,2,0:T(8,128)(2,1)S(1)}, bf16[1,192,48]{1,2,0:T(8,128)(2,1)}, u32[]{:S(2)}) copy-start(bf16[1,192,48]{1,2,0:T(8,128)(2,1)} %param.20) | copy-start | bytes 55300
  55.4 14.5 %copy-start.9 = (bf16[1,192,192]{2,1,0:T(8,128)(2,1)S(1)}, bf16[1,192,192]{2,1,0:T(8,128)(2,1)}, u32[]{:S(2)}) copy-start(bf16[1,192,192]{2,1,0:T(8,128)(2,1)} %param.26) | copy-start | bytes 221188
  60.3 69.4 %copy-start.16 = (f32[192]{0:T(256)}, f32[192]{0:T(256)S(1)}, u32[]{:S(2)}) copy-start(f32[192]{0:T(256)S(1)} %add.316) | copy-start | bytes 2308
  60.3 70.0 %copy-start.18 = (f32[768]{0:T(1024)}, f32[768]{0:T(1024)S(1)}, u32[]{:S(2)}) copy-start(f32[768]{0:T(1024)S(1)} %add.317) | copy-start | bytes 9220
  60.3 70.0 %copy-start.30 = (f32[192]{0:T(256)}, f32[192]{0:T(256)S(1)}, u32[]{:S(2)}) copy-start(f32[192]{0:T(256)S(1)} %add.318) | copy-start | bytes 2308
  60.8 69.5 %copy-start.24 = (f32[1,192]{1,0:T(1,128)}, f32[1,192]{1,0:T(1,128)S(1)}, u32[]{:S(2)}) copy-start(f32[1,192]{1,0:T(1,128)S(1)} %mul.170) | copy-start | bytes 2308
  60.9 69.4 %copy-start.26 = (f32[1,192]{1,0:T(1,128)}, f32[1,192]{1,0:T(1,128)S(1)}, u32[]{:S(2)}) copy-start(f32[1,192]{1,0:T(1,128)S(1)} %add.304) | copy-start | bytes 2308
  81.1 15.4 %collective-permute-start = (bf16[288,384]{1,0:T(8,128)(2,1)S(1)}, bf16[288,384]{1,0:T(8,128)(2,1)}, u32[]{:S(2)}, u32[]{:S(2)}) collective-permute-start(bf16[288,384]{1,0:T(8,128)(2,1)S(1)} %slice.62), channel_id=1, source_target_pairs={{0,4},{4,0},{8,12},{12,8},{16,20},{20,16},{24,28},{28,24},{32,36},... | collective-permute-start | bytes 663560 | tf_op jit(solution)/shard_map/ppermute | solution.py:20
  99.4 1.1 copy-start.4
  103.7 1.9 %copy-start.1 = (bf16[1,768,192]{2,1,0:T(8,128)(2,1)S(1)}, bf16[1,768,192]{2,1,0:T(8,128)(2,1)}, u32[]{:S(2)}) copy-start(bf16[1,768,192]{2,1,0:T(8,128)(2,1)} %all_gather.26) | copy-start | bytes 884740
  105.6 11.5 %copy-start.13 = (f32[1,192]{1,0:T(1,128)S(1)}, f32[1,192]{1,0:T(1,128)}, u32[]{:S(2)}) copy-start(f32[1,192]{1,0:T(1,128)} %copy-done.12) | copy-start | bytes 2308
  105.6 11.5 %copy-start.15 = (f32[1,192]{1,0:T(1,128)S(1)}, f32[1,192]{1,0:T(1,128)}, u32[]{:S(2)}) copy-start(f32[1,192]{1,0:T(1,128)} %copy-done.14) | copy-start | bytes 2308
  108.0 13.1 %copy-start.5 = (bf16[288,192]{1,0:T(8,128)(2,1)}, bf16[288,192]{1,0:T(8,128)(2,1)S(1)}, u32[]{:S(2)}) copy-start(bf16[288,192]{1,0:T(8,128)(2,1)S(1)} %fusion.17) | copy-start | bytes 331780
  108.0 8.8 %collective-permute-start.1 = (bf16[2,3,48,192]{3,2,1,0:T(8,128)(2,1)S(1)}, bf16[2,3,48,192]{3,2,1,0:T(8,128)(2,1)S(1)}, u32[]{:S(2)}, u32[]{:S(2)}) collective-permute-start(bf16[2,3,48,192]{3,2,1,0:T(8,128)(2,1)S(1)} %bitcast.160), channel_id=1, source_target_pairs={{0,256},{1,257},{2,258},{3,259},{4,260},{5,261},{6,262},{7,263},{8... | collective-permute-start | bytes 331784 | tf_op jit(solution)/shard_map/ppermute | solution.py:26
  117.7 4.2 %collective-permute-start.2 = (bf16[288,384]{1,0:T(8,128)(2,1)S(1)}, bf16[288,384]{1,0:T(8,128)(2,1)}, u32[]{:S(2)}, u32[]{:S(2)}) collective-permute-start(bf16[288,384]{1,0:T(8,128)(2,1)S(1)} %slice.66), channel_id=1, source_target_pairs={{0,4},{4,0},{8,12},{12,8},{16,20},{20,16},{24,28},{28,24},{32,36},... | collective-permute-start | bytes 663560 | tf_op jit(solution)/shard_map/ppermute | solution.py:20
  128.4 2.0 %copy-start.2 = (bf16[1,768,192]{2,1,0:T(8,128)(2,1)S(1)}, bf16[1,768,192]{2,1,0:T(8,128)(2,1)}, u32[]{:S(2)}) copy-start(bf16[1,768,192]{2,1,0:T(8,128)(2,1)} %all_gather.26) | copy-start | bytes 884740
  132.7 13.0 %copy-start.7 = (bf16[288,192]{1,0:T(8,128)(2,1)}, bf16[288,192]{1,0:T(8,128)(2,1)S(1)}, u32[]{:S(2)}) copy-start(bf16[288,192]{1,0:T(8,128)(2,1)S(1)} %fusion.16) | copy-start | bytes 331780
  132.7 8.5 %collective-permute-start.3 = (bf16[2,3,48,192]{3,2,1,0:T(8,128)(2,1)S(1)}, bf16[2,3,48,192]{3,2,1,0:T(8,128)(2,1)S(1)}, u32[]{:S(2)}, u32[]{:S(2)}) collective-permute-start(bf16[2,3,48,192]{3,2,1,0:T(8,128)(2,1)S(1)} %bitcast.162), channel_id=1, source_target_pairs={{0,256},{1,257},{2,258},{3,259},{4,260},{5,261},{6,262},{7,263},{8... | collective-permute-start | bytes 331784 | tf_op jit(solution)/shard_map/ppermute | solution.py:26
  142.2 4.2 %collective-permute-start.4 = (bf16[288,384]{1,0:T(8,128)(2,1)S(1)}, bf16[288,384]{1,0:T(8,128)(2,1)S(1)}, u32[]{:S(2)}, u32[]{:S(2)}) collective-permute-start(bf16[288,384]{1,0:T(8,128)(2,1)S(1)} %slice.70), channel_id=1, source_target_pairs={{0,4},{4,0},{8,12},{12,8},{16,20},{20,16},{24,28},{28,24},{32,36},... | collective-permute-start | bytes 663560 | tf_op jit(solution)/shard_map/ppermute | solution.py:20
  148.4 1.1 copy-start.3
  152.6 1.4 copy-start.17
  152.7 2.0 %copy-start.19 = (f32[768]{0:T(1024)S(1)}, f32[768]{0:T(1024)}, u32[]{:S(2)}) copy-start(f32[768]{0:T(1024)} %copy-done.18) | copy-start | bytes 9220
  152.7 2.0 %copy-start.25 = (f32[1,192]{1,0:T(1,128)S(1)}, f32[1,192]{1,0:T(1,128)}, u32[]{:S(2)}) copy-start(f32[1,192]{1,0:T(1,128)} %copy-done.24) | copy-start | bytes 2308
  152.7 2.0 %copy-start.27 = (f32[1,192]{1,0:T(1,128)S(1)}, f32[1,192]{1,0:T(1,128)}, u32[]{:S(2)}) copy-start(f32[1,192]{1,0:T(1,128)} %copy-done.26) | copy-start | bytes 2308
  152.7 2.0 %copy-start.31 = (f32[192]{0:T(256)S(1)}, f32[192]{0:T(256)}, u32[]{:S(2)}) copy-start(f32[192]{0:T(256)} %copy-done.30) | copy-start | bytes 2308
  154.7 2.4 %copy-start.6 = (bf16[288,192]{1,0:T(8,128)(2,1)S(1)}, bf16[288,192]{1,0:T(8,128)(2,1)}, u32[]{:S(2)}) copy-start(bf16[288,192]{1,0:T(8,128)(2,1)} %copy-done.5) | copy-start | bytes 331780
  154.7 2.4 %copy-start.8 = (bf16[288,192]{1,0:T(8,128)(2,1)S(1)}, bf16[288,192]{1,0:T(8,128)(2,1)}, u32[]{:S(2)}) copy-start(bf16[288,192]{1,0:T(8,128)(2,1)} %copy-done.7) | copy-start | bytes 331780
